TPU v7x, 256 devices: a whole 4x4x8 slice. The times are simulated.
256 devices in a mesh: ctx: 32 (over y_hi, z, core), ch: 8 (over x, y_lo).
Axes of the slice: x: 4, y: 4 (y_hi: 2, y_lo: 2; y = y_hi * 2 + y_lo), z: 8, core: 2. Of those that a mesh axis runs over, the one named last changes fastest.
Arguments:
- activations: bfloat16 [2, 4096, 8192], P(None, 'ctx', 'ch'), may hold values from -62 to 62
- grad_in: bfloat16 [2, 4096, 8192], P(None, 'ctx', 'ch'), may hold values from -6 to 6
- gate_out: bfloat16 [3, 2, 4096, 8192], P(None, None, 'ctx', 'ch'), may hold values from -6 to 6
- gate_in: bfloat16 [3, 2, 4096, 8192], P(None, None, 'ctx', 'ch'), may hold values from -6 to 6
- filters: bfloat16 [3, 512, 128], P(None, 'ch'), may hold values from -0.5 to 0.5
Outputs:
- grad_input: bfloat16 [2, 4096, 8192], P(None, 'ctx', 'ch')
- grad_gate_out: bfloat16 [3, 2, 4096, 8192], P(None, None, 'ctx', 'ch')
- grad_gate_in: bfloat16 [3, 2, 4096, 8192], P(None, None, 'ctx', 'ch')
- grad_filters: float32 [3, 512, 128], P(None, 'ch', 'ctx')
All inputs are finite; a program needn't handle non-finite values.
Results may differ from a plain program's by a relative error of at most 0.023.
Values may be sent and summed in bfloat16 or wider, within the bound.
A program may use at most 128 MiB of HBM per device.

v0:
```python
import jax
import jax.numpy as jnp
from jax import lax
from jax.sharding import PartitionSpec as P

D = 8192
GROUP = 16
LAYERS = 3


def partner(block, axis, apart):
    count = lax.axis_size(axis)
    route = []
    for low in range(count):
        high = low | 1 << apart
        if high != low and high < count:
            route += [(low, high), (high, low)]
    return lax.ppermute(block, axis, route)


def shifted(value, axis, steps):
    count = lax.axis_size(axis)
    leading, last = (max(0, -steps), min(count, count - steps))
    return lax.ppermute(value, axis, [(source, source + steps) for source in range(leading, last)])


def arrive_paired(folded):
    half_rows = folded.shape[1] // 2
    bit_count = lax.axis_size("ctx").bit_length() - 1
    own_index = lax.axis_index("ctx")
    leading = folded[:, :half_rows]
    trailing = folded[:, half_rows:]
    for bit_index in range(bit_count):
        trailing = partner(trailing, "ctx", bit_index)
    for bit_index in reversed(range(bit_count)):
        lower = own_index // 2**bit_index % 2 == 0
        outgoing = jnp.where(lower, trailing, leading)
        incoming = partner(outgoing, "ctx", bit_index)
        leading, trailing = (
            jnp.where(lower, leading, incoming),
            jnp.where(lower, incoming, trailing),
        )
    return jnp.concatenate([leading, trailing], axis=1)


def leave_paired(ordered):
    half_rows = ordered.shape[1] // 2
    bit_count = lax.axis_size("ctx").bit_length() - 1
    own_index = lax.axis_index("ctx")
    leading = ordered[:, :half_rows]
    trailing = ordered[:, half_rows:]
    for bit_index in range(bit_count):
        lower = own_index // 2**bit_index % 2 == 0
        outgoing = jnp.where(lower, trailing, leading)
        incoming = partner(outgoing, "ctx", bit_index)
        leading, trailing = (
            jnp.where(lower, leading, incoming),
            jnp.where(lower, incoming, trailing),
        )
    for bit_index in range(bit_count):
        trailing = partner(trailing, "ctx", bit_index)
    return jnp.concatenate([leading, trailing], axis=1)


def local(activations, grad_in, gate_out, gate_in, filters):
    seq_count, row_count, width_local = activations.shape
    tap_count = filters.shape[2]
    group_count = width_local // GROUP
    ext_rows = row_count + tap_count - 1
    lead_pos = lax.broadcasted_iota(jnp.int32, (row_count, ext_rows, tap_count), 0)
    col_pos = lax.broadcasted_iota(jnp.int32, (row_count, ext_rows, tap_count), 1)
    lag_pos = lax.broadcasted_iota(jnp.int32, (row_count, ext_rows, tap_count), 2)
    ahead_hot = (col_pos - lead_pos == tap_count - 1 - lag_pos).astype(jnp.bfloat16)
    behind_hot = (col_pos - lead_pos == lag_pos).astype(jnp.bfloat16)
    ahead_float = ahead_hot.astype(jnp.float32)
    current = activations
    saved = []
    for layer_index in range(LAYERS):
        taps_local = filters[layer_index]
        toeplitz = jnp.einsum(
            "tjs,gs->gtj", ahead_hot, taps_local, preferred_element_type=jnp.float32
        ).astype(jnp.bfloat16)
        values = current.astype(jnp.float32)
        sum_squares = lax.psum(jnp.sum(values * values, axis=2), "ch")
        inverse_rms = lax.rsqrt(sum_squares / D + 1e-06)[..., None]
        normed = values * inverse_rms
        inputs = (gate_in[layer_index].astype(jnp.float32) * normed).astype(jnp.bfloat16)
        earlier = shifted(inputs[:, row_count - tap_count + 1 :, :], "ctx", 1)
        inputs_ext = jnp.concatenate([earlier, inputs], axis=1).reshape(
            seq_count, ext_rows, group_count, GROUP
        )
        filtered = jnp.einsum(
            "gtj,sjgc->stgc", toeplitz, inputs_ext, preferred_element_type=jnp.float32
        ).reshape(seq_count, row_count, width_local)
        saved.append((inverse_rms, normed, inputs_ext, filtered))
        if layer_index + 1 < LAYERS:
            current = (gate_out[layer_index].astype(jnp.float32) * filtered).astype(jnp.bfloat16)
    gradient = arrive_paired(grad_in)
    out_grads = [None] * LAYERS
    in_grads = [None] * LAYERS
    filter_grads = [None] * LAYERS
    for layer_index in reversed(range(LAYERS)):
        inverse_rms, normed, inputs_ext, filtered = saved[layer_index]
        back_toeplitz = jnp.einsum(
            "jts,gs->gjt", behind_hot, filters[layer_index], preferred_element_type=jnp.float32
        ).astype(jnp.bfloat16)
        incoming = gradient.astype(jnp.float32)
        out_grads[layer_index] = (incoming * filtered).astype(jnp.bfloat16)
        gated = (gate_out[layer_index].astype(jnp.float32) * incoming).astype(jnp.bfloat16)
        later = shifted(gated[:, : tap_count - 1, :], "ctx", -1)
        gated_ext = jnp.concatenate([gated, later], axis=1).reshape(
            seq_count, ext_rows, group_count, GROUP
        )
        spread_back = jnp.einsum(
            "gjt,stgc->sjgc", back_toeplitz, gated_ext, preferred_element_type=jnp.float32
        ).reshape(seq_count, row_count, width_local)
        pair_sums = jnp.einsum(
            "stgc,sjgc->gtj",
            gated.reshape(seq_count, row_count, group_count, GROUP),
            inputs_ext,
            preferred_element_type=jnp.float32,
        )
        local_taps = jnp.einsum(
            "gtj,tjs->gs",
            pair_sums,
            ahead_float,
            precision=lax.Precision.HIGHEST,
            preferred_element_type=jnp.float32,
        )
        filter_grads[layer_index] = lax.psum_scatter(
            local_taps.astype(jnp.bfloat16), "ctx", scatter_dimension=1, tiled=True
        ).astype(jnp.float32)
        in_grads[layer_index] = (spread_back * normed).astype(jnp.bfloat16)
        grad_normed = spread_back * gate_in[layer_index].astype(jnp.float32)
        inner = lax.psum(jnp.sum(grad_normed * normed, axis=2), "ch")
        gradient = (inverse_rms * (grad_normed - normed * (inner / D)[..., None])).astype(
            jnp.bfloat16
        )
    grad_filters = jnp.stack(filter_grads)
    grad_input = leave_paired(gradient)
    return (grad_input, jnp.stack(out_grads), jnp.stack(in_grads), grad_filters)


def solution(mesh):
    return jax.shard_map(
        local,
        mesh=mesh,
        in_specs=(
            P(None, "ctx", "ch"),
            P(None, "ctx", "ch"),
            P(None, None, "ctx", "ch"),
            P(None, None, "ctx", "ch"),
            P(None, "ch", None),
        ),
        out_specs=(
            P(None, "ctx", "ch"),
            P(None, None, "ctx", "ch"),
            P(None, None, "ctx", "ch"),
            P(None, "ch", "ctx"),
        ),
        check_vma=False,
    )
```

profile of v0, /device:TPU:16, one launch (start us, length us, event | category | flops | bytes accessed | tf_op | source)
XLA Modules:
  0.0 630.8 jit_solution(11319060025518432840)
XLA Ops:
  8.4 9.7 %collective-permute-done.3 = bf16[2,64,1024]{1,2,0:T(8,128)(2,1)S(1)} collective-permute-done((bf16[2,64,1024]{1,2,0:T(8,128)(2,1)S(1)}, bf16[2,64,1024]{1,2,0:T(8,128)(2,1)S(1)}, u32[]{:S(2)}, u32[]{:S(2)}) %collective-permute-start.3) | collective-permute-done | bytes 262176 | tf_op jit(solution)/shard_map/ppermute | solution.py:18
  21.8 19.4 %psum.42 = f32[2,128]{1,0:T(2,128)S(1)} all-reduce(f32[2,128]{1,0:T(2,128)S(1)} %fusion.111), channel_id=1, replica_groups=mesh['ctx'=32,'ch'=8] {'ch'}, use_global_device_ids=true, to_apply=%region_1.0 | all-reduce | flops 256 | bytes 2048 | tf_op jit(solution)/shard_map/psum | solution.py:84
  44.2 6.2 collective-permute-start.5
  53.9 20.4 %collective-permute-done.5 = bf16[2,64,1024]{1,2,0:T(8,128)(2,1)} collective-permute-done((bf16[2,64,1024]{1,2,0:T(8,128)(2,1)S(1)}, bf16[2,64,1024]{1,2,0:T(8,128)(2,1)}, u32[]{:S(2)}, u32[]{:S(2)}) %collective-permute-start.5) | collective-permute-done | bytes 262176 | tf_op jit(solution)/shard_map/ppermute | solution.py:18
  80.6 7.1 %collective-permute-done.6 = bf16[2,64,1024]{1,2,0:T(8,128)(2,1)S(1)} collective-permute-done((bf16[2,64,1024]{1,2,0:T(8,128)(2,1)}, bf16[2,64,1024]{1,2,0:T(8,128)(2,1)S(1)}, u32[]{:S(2)}, u32[]{:S(2)}) %collective-permute-start.6) | collective-permute-done | bytes 262176 | tf_op jit(solution)/shard_map/ppermute | solution.py:18
  93.9 6.3 collective-permute-done.7
  107.7 11.3 %collective-permute-done.8 = bf16[2,64,1024]{1,2,0:T(8,128)(2,1)} collective-permute-done((bf16[2,64,1024]{1,2,0:T(8,128)(2,1)}, bf16[2,64,1024]{1,2,0:T(8,128)(2,1)}, u32[]{:S(2)}, u32[]{:S(2)}) %collective-permute-start.8) | collective-permute-done | bytes 262176 | tf_op jit(solution)/shard_map/ppermute | solution.py:18
  132.8 19.3 %psum.43 = f32[2,128]{1,0:T(2,128)S(1)} all-reduce(f32[2,128]{1,0:T(2,128)S(1)} %get-tuple-element.23), channel_id=1, replica_groups=mesh['ctx'=32,'ch'=8] {'ch'}, use_global_device_ids=true, to_apply=%region_3.0 | all-reduce | flops 256 | bytes 2048 | tf_op jit(solution)/shard_map/psum | solution.py:84
  188.7 20.4 %psum.44 = f32[2,128]{1,0:T(2,128)S(1)} all-reduce(f32[2,128]{1,0:T(2,128)S(1)} %get-tuple-element.21), channel_id=1, replica_groups=mesh['ctx'=32,'ch'=8] {'ch'}, use_global_device_ids=true, to_apply=%region_5.0 | all-reduce | flops 256 | bytes 2048 | tf_op jit(solution)/shard_map/psum | solution.py:84
  210.5 6.7 %fusion.98 = (f32[2,128]{1,0:T(2,128)S(1)}, f32[2,128,64,16]{1,3,0,2:T(8,128)S(1)}) fusion(bf16[2,128,64,16]{1,3,0,2:T(8,128)(2,1)} %get-tuple-element.22, f32[2,128]{1,0:T(2,128)S(1)} %add_rsqrt_fusion, bf16[64,128,255,1]{1,0,2,3:T(8,128)(2,1)} %convert_bitcast_fusion.3, bf16[2,255,64,16]{1,3,2,0:T(8,128)(2,1)S(1)} %bitcast.263, ...), kind=kOutput, calls=%fused_computation.71 | convolution fusion | flops 135266048 | bytes 7321600 | tf_op jit(solution)/shard_map/gjt,stgc->sjgc/dot_general | solution.py:114
  219.2 15.9 %psum.45 = f32[2,128]{1,0:T(2,128)S(1)} all-reduce(f32[2,128]{1,0:T(2,128)S(1)} %get-tuple-element.53), channel_id=1, replica_groups=mesh['ctx'=32,'ch'=8] {'ch'}, use_global_device_ids=true, to_apply=%region_7.8 | all-reduce | flops 256 | bytes 2048 | tf_op jit(solution)/shard_map/psum | solution.py:135
  253.3 17.9 %psum.46 = f32[2,128]{1,0:T(2,128)S(1)} all-reduce(f32[2,128]{1,0:T(2,128)S(1)} %get-tuple-element.55), channel_id=1, replica_groups=mesh['ctx'=32,'ch'=8] {'ch'}, use_global_device_ids=true, to_apply=%region_9.10 | all-reduce | flops 256 | bytes 2048 | tf_op jit(solution)/shard_map/psum | solution.py:135
  290.8 17.0 %psum.47 = f32[2,128]{1,0:T(2,128)S(1)} all-reduce(f32[2,128]{1,0:T(2,128)S(1)} %get-tuple-element.38), channel_id=1, replica_groups=mesh['ctx'=32,'ch'=8] {'ch'}, use_global_device_ids=true, to_apply=%region_11.12 | all-reduce | flops 256 | bytes 2048 | tf_op jit(solution)/shard_map/psum | solution.py:135
  310.1 15.9 %fusion.88 = bf16[64,128]{0,1:T(8,128)(2,1)S(1)} fusion(s32[128]{0:T(128)S(1)} %iota_subtract_fusion.1, f32[64,128,255]{1,2,0:T(8,128)} %convolution_bitcast_fusion.1), kind=kOutput, calls=%fused_computation.69 | convolution fusion | flops 3217006592 | bytes 8372736 | tf_op jit(solution)/shard_map/gtj,tjs->gs/dot_general | solution.py:123
  330.8 12.4 %collective-permute-done.16 = bf16[2,64,1024]{1,2,0:T(8,128)(2,1)S(1)} collective-permute-done((bf16[2,64,1024]{1,2,0:T(8,128)(2,1)S(1)}, bf16[2,64,1024]{1,2,0:T(8,128)(2,1)S(1)}, u32[]{:S(2)}, u32[]{:S(2)}) %collective-permute-start.16) | collective-permute-done | bytes 262176 | tf_op jit(solution)/shard_map/ppermute | solution.py:18
  344.7 25.1 %collective-permute-done.17 = bf16[2,64,1024]{1,2,0:T(8,128)(2,1)S(1)} collective-permute-done((bf16[2,64,1024]{1,2,0:T(8,128)(2,1)S(1)}, bf16[2,64,1024]{1,2,0:T(8,128)(2,1)S(1)}, u32[]{:S(2)}, u32[]{:S(2)}) %collective-permute-start.17) | collective-permute-done | bytes 262176 | tf_op jit(solution)/shard_map/ppermute | solution.py:18
  373.7 18.8 %fusion.93 = bf16[64,128]{0,1:T(8,128)(2,1)S(1)} fusion(s32[128]{0:T(128)S(1)} %iota_subtract_fusion.1, f32[64,128,255]{1,2,0:T(8,128)S(1)} %convolution_bitcast_fusion.2), kind=kOutput, calls=%fused_computation.70 | convolution fusion | flops 3217006592 | bytes 8372736 | tf_op jit(solution)/shard_map/gtj,tjs->gs/dot_general | solution.py:123
  392.6 6.8 %collective-permute-done.18 = bf16[2,64,1024]{1,2,0:T(8,128)(2,1)S(1)} collective-permute-done((bf16[2,64,1024]{1,2,0:T(8,128)(2,1)S(1)}, bf16[2,64,1024]{1,2,0:T(8,128)(2,1)S(1)}, u32[]{:S(2)}, u32[]{:S(2)}) %collective-permute-start.18) | collective-permute-done | bytes 262176 | tf_op jit(solution)/shard_map/ppermute | solution.py:18
  401.7 12.8 %collective-permute-done.19 = bf16[2,64,1024]{1,2,0:T(8,128)(2,1)S(1)} collective-permute-done((bf16[2,64,1024]{1,2,0:T(8,128)(2,1)S(1)}, bf16[2,64,1024]{1,2,0:T(8,128)(2,1)S(1)}, u32[]{:S(2)}, u32[]{:S(2)}) %collective-permute-start.19) | collective-permute-done | bytes 262176 | tf_op jit(solution)/shard_map/ppermute | solution.py:18
  415.6 18.9 %fusion.83 = bf16[64,128]{0,1:T(8,128)(2,1)S(1)} fusion(s32[128]{0:T(128)S(1)} %iota_subtract_fusion.1, f32[64,128,255]{1,2,0:T(8,128)S(1)} %convolution_bitcast_fusion), kind=kOutput, calls=%fused_computation.68 | convolution fusion | flops 3217006592 | bytes 8372736 | tf_op jit(solution)/shard_map/gtj,tjs->gs/dot_general | solution.py:123
  439.9 129.8 %all-reduce.3 = (bf16[64,128]{0,1:T(8,128)(2,1)S(1)}, bf16[64,128]{0,1:T(8,128)(2,1)S(1)}, bf16[64,128]{0,1:T(8,128)(2,1)S(1)}) all-reduce(bf16[64,128]{0,1:T(8,128)(2,1)S(1)} %fusion.83, bf16[64,128]{0,1:T(8,128)(2,1)S(1)} %fusion.88, bf16[64,128]{0,1:T(8,128)(2,1)S(1)} %fusion.93), channel_id=4, replica_groups=mesh['ctx'=32,'ch'=8] {'ctx'}, use_global_device_ids=true, to_apply=%region_14.15.clone | all-reduce | flops 24576 | bytes 98304
  570.4 15.9 %collective-permute-done.22 = bf16[2,64,1024]{1,2,0:T(8,128)(2,1)S(1)} collective-permute-done((bf16[2,64,1024]{1,2,0:T(8,128)(2,1)}, bf16[2,64,1024]{1,2,0:T(8,128)(2,1)S(1)}, u32[]{:S(2)}, u32[]{:S(2)}) %collective-permute-start.22) | collective-permute-done | bytes 262176 | tf_op jit(solution)/shard_map/ppermute | solution.py:18
  586.7 26.4 %collective-permute-done.23 = bf16[2,64,1024]{1,2,0:T(8,128)(2,1)} collective-permute-done((bf16[2,64,1024]{1,2,0:T(8,128)(2,1)S(1)}, bf16[2,64,1024]{1,2,0:T(8,128)(2,1)}, u32[]{:S(2)}, u32[]{:S(2)}) %collective-permute-start.23) | collective-permute-done | bytes 262176 | tf_op jit(solution)/shard_map/ppermute | solution.py:18
  618.9 8.9 %collective-permute-done.24 = bf16[2,64,1024]{1,2,0:T(8,128)(2,1)} collective-permute-done((bf16[2,64,1024]{1,2,0:T(8,128)(2,1)}, bf16[2,64,1024]{1,2,0:T(8,128)(2,1)}, u32[]{:S(2)}, u32[]{:S(2)}) %collective-permute-start.24) | collective-permute-done | bytes 262176 | tf_op jit(solution)/shard_map/ppermute | solution.py:18
  (209 shorter events, 158.7 us)
Async XLA Ops:
  4.0 14.1 %collective-permute-start.3 = (bf16[2,64,1024]{1,2,0:T(8,128)(2,1)S(1)}, bf16[2,64,1024]{1,2,0:T(8,128)(2,1)S(1)}, u32[]{:S(2)}, u32[]{:S(2)}) collective-permute-start(bf16[2,64,1024]{1,2,0:T(8,128)(2,1)S(1)} %collective-permute-done.2), channel_id=1, source_target_pairs={{0,16},{16,0},{8,24},{24,8},{32,48},{48,32},{40,56},{56,40},{64,80... | collective-permute-start | bytes 786440 | tf_op jit(solution)/shard_map/ppermute | solution.py:18
  18.1 26.0 %collective-permute-start.4 = (bf16[2,64,1024]{1,2,0:T(8,128)(2,1)S(1)}, bf16[2,64,1024]{1,2,0:T(8,128)(2,1)S(1)}, u32[]{:S(2)}, u32[]{:S(2)}) collective-permute-start(bf16[2,64,1024]{1,2,0:T(8,128)(2,1)S(1)} %collective-permute-done.3), channel_id=1, source_target_pairs={{0,32},{32,0},{8,40},{40,8},{16,48},{48,16},{24,56},{56,24},{64,96... | collective-permute-start | bytes 786440 | tf_op jit(solution)/shard_map/ppermute | solution.py:18
  44.2 30.1 %collective-permute-start.5 = (bf16[2,64,1024]{1,2,0:T(8,128)(2,1)S(1)}, bf16[2,64,1024]{1,2,0:T(8,128)(2,1)}, u32[]{:S(2)}, u32[]{:S(2)}) collective-permute-start(bf16[2,64,1024]{1,2,0:T(8,128)(2,1)S(1)} %collective-permute-done.4), channel_id=1, source_target_pairs={{0,64},{64,0},{8,72},{72,8},{16,80},{80,16},{24,88},{88,24},{32,96... | collective-permute-start | bytes 786440 | tf_op jit(solution)/shard_map/ppermute | solution.py:18
  51.6 54.3 %collective-permute-start = (bf16[2,127,1024]{1,2,0:T(8,128)(2,1)}, bf16[2,127,1024]{1,2,0:T(8,128)(2,1)}, u32[]{:S(2)}, u32[]{:S(2)}) collective-permute-start(bf16[2,127,1024]{1,2,0:T(8,128)(2,1)} %slice.84), channel_id=1, source_target_pairs={{0,8},{8,16},{16,24},{24,32},{32,40},{40,48},{48,56},{56,64},{64,7... | collective-permute-start | bytes 1560584 | tf_op jit(solution)/shard_map/ppermute | solution.py:24
  74.3 13.4 %collective-permute-start.6 = (bf16[2,64,1024]{1,2,0:T(8,128)(2,1)}, bf16[2,64,1024]{1,2,0:T(8,128)(2,1)S(1)}, u32[]{:S(2)}, u32[]{:S(2)}) collective-permute-start(bf16[2,64,1024]{1,2,0:T(8,128)(2,1)} %collective-permute-done.5), channel_id=1, source_target_pairs={{0,128},{128,0},{8,136},{136,8},{16,144},{144,16},{24,152},{152,24... | collective-permute-start | bytes 786440 | tf_op jit(solution)/shard_map/ppermute | solution.py:18
  87.8 12.4 %collective-permute-start.7 = (bf16[2,64,1024]{1,2,0:T(8,128)(2,1)S(1)}, bf16[2,64,1024]{1,2,0:T(8,128)(2,1)S(1)}, u32[]{:S(2)}, u32[]{:S(2)}) collective-permute-start(bf16[2,64,1024]{1,2,0:T(8,128)(2,1)S(1)} %broadcast_select_fusion.29), channel_id=1, source_target_pairs={{0,128},{128,0},{8,136},{136,8},{16,144},{144,16},{24,152},{152,24... | collective-permute-start | bytes 786440 | tf_op jit(solution)/shard_map/ppermute | solution.py:18
  101.2 17.8 %collective-permute-start.8 = (bf16[2,64,1024]{1,2,0:T(8,128)(2,1)}, bf16[2,64,1024]{1,2,0:T(8,128)(2,1)}, u32[]{:S(2)}, u32[]{:S(2)}) collective-permute-start(bf16[2,64,1024]{1,2,0:T(8,128)(2,1)} %broadcast_select_fusion.23), channel_id=1, source_target_pairs={{0,64},{64,0},{8,72},{72,8},{16,80},{80,16},{24,88},{88,24},{32,96... | collective-permute-start | bytes 786440 | tf_op jit(solution)/shard_map/ppermute | solution.py:18
  121.6 30.4 %collective-permute-start.9 = (bf16[2,64,1024]{1,2,0:T(8,128)(2,1)}, bf16[2,64,1024]{1,2,0:T(8,128)(2,1)}, u32[]{:S(2)}, u32[]{:S(2)}) collective-permute-start(bf16[2,64,1024]{1,2,0:T(8,128)(2,1)} %get-tuple-element.28), channel_id=1, source_target_pairs={{0,32},{32,0},{8,40},{40,8},{16,48},{48,16},{24,56},{56,24},{64,96... | collective-permute-start | bytes 786440 | tf_op jit(solution)/shard_map/ppermute | solution.py:18
  153.4 9.3 %collective-permute-start.10 = (bf16[2,64,1024]{1,2,0:T(8,128)(2,1)S(1)}, bf16[2,64,1024]{1,2,0:T(8,128)(2,1)S(1)}, u32[]{:S(2)}, u32[]{:S(2)}) collective-permute-start(bf16[2,64,1024]{1,2,0:T(8,128)(2,1)S(1)} %broadcast_select_fusion.11), channel_id=1, source_target_pairs={{0,16},{16,0},{8,24},{24,8},{32,48},{48,32},{40,56},{56,40},{64,80... | collective-permute-start | bytes 786440 | tf_op jit(solution)/shard_map/ppermute | solution.py:18
  155.5 19.7 %collective-permute-start.1 = (bf16[2,127,1024]{1,2,0:T(8,128)(2,1)}, bf16[2,127,1024]{1,2,0:T(8,128)(2,1)}, u32[]{:S(2)}, u32[]{:S(2)}) collective-permute-start(bf16[2,127,1024]{1,2,0:T(8,128)(2,1)} %slice.85), channel_id=1, source_target_pairs={{0,8},{8,16},{16,24},{24,32},{32,40},{40,48},{48,56},{56,64},{64,7... | collective-permute-start | bytes 1560584 | tf_op jit(solution)/shard_map/ppermute | solution.py:24
  165.1 11.9 %collective-permute-start.11 = (bf16[2,64,1024]{1,2,0:T(8,128)(2,1)}, bf16[2,64,1024]{1,2,0:T(8,128)(2,1)}, u32[]{:S(2)}, u32[]{:S(2)}) collective-permute-start(bf16[2,64,1024]{1,2,0:T(8,128)(2,1)} %get-tuple-element.25), channel_id=1, source_target_pairs={{0,8},{8,0},{16,24},{24,16},{32,40},{40,32},{48,56},{56,48},{64,72... | collective-permute-start | bytes 786440 | tf_op jit(solution)/shard_map/ppermute | solution.py:18
  180.7 28.4 %collective-permute-start.12 = (bf16[2,127,1024]{1,2,0:T(8,128)(2,1)}, bf16[2,127,1024]{1,2,0:T(8,128)(2,1)}, u32[]{:S(2)}, u32[]{:S(2)}) collective-permute-start(bf16[2,127,1024]{1,2,0:T(8,128)(2,1)} %bitcast.237), channel_id=1, source_target_pairs={{8,0},{16,8},{24,16},{32,24},{40,32},{48,40},{56,48},{64,56},{72,6... | collective-permute-start | bytes 1560584 | tf_op jit(solution)/shard_map/ppermute | solution.py:24
  238.0 9.9 %collective-permute-start.13 = (bf16[2,127,1024]{1,2,0:T(8,128)(2,1)S(1)}, bf16[2,127,1024]{1,2,0:T(8,128)(2,1)S(1)}, u32[]{:S(2)}, u32[]{:S(2)}) collective-permute-start(bf16[2,127,1024]{1,2,0:T(8,128)(2,1)S(1)} %bitcast.262), channel_id=1, source_target_pairs={{8,0},{16,8},{24,16},{32,24},{40,32},{48,40},{56,48},{64,56},{72,6... | collective-permute-start | bytes 1560584 | tf_op jit(solution)/shard_map/ppermute | solution.py:24
  309.6 19.4 %collective-permute-start.15 = (bf16[2,64,1024]{1,2,0:T(8,128)(2,1)S(1)}, bf16[2,64,1024]{1,2,0:T(8,128)(2,1)S(1)}, u32[]{:S(2)}, u32[]{:S(2)}) collective-permute-start(bf16[2,64,1024]{1,2,0:T(8,128)(2,1)S(1)} %broadcast_select_fusion.2), channel_id=1, source_target_pairs={{0,8},{8,0},{16,24},{24,16},{32,40},{40,32},{48,56},{56,48},{64,72... | collective-permute-start | bytes 786440 | tf_op jit(solution)/shard_map/ppermute | solution.py:18
  326.3 73.3 %collective-permute-start.25 = (bf16[2,127,1024]{1,2,0:T(8,128)(2,1)S(1)}, bf16[2,127,1024]{1,2,0:T(8,128)(2,1)S(1)}, u32[]{:S(2)}, u32[]{:S(2)}) collective-permute-start(bf16[2,127,1024]{1,2,0:T(8,128)(2,1)S(1)} %slice.91), channel_id=1, source_target_pairs={{0,8},{8,16},{16,24},{24,32},{32,40},{40,48},{48,56},{56,64},{64,7... | collective-permute-start | bytes 1560584 | tf_op jit(solution)/shard_map/ppermute | solution.py:24
  329.2 13.9 %collective-permute-start.16 = (bf16[2,64,1024]{1,2,0:T(8,128)(2,1)S(1)}, bf16[2,64,1024]{1,2,0:T(8,128)(2,1)S(1)}, u32[]{:S(2)}, u32[]{:S(2)}) collective-permute-start(bf16[2,64,1024]{1,2,0:T(8,128)(2,1)S(1)} %get-tuple-element.18), channel_id=1, source_target_pairs={{0,16},{16,0},{8,24},{24,8},{32,48},{48,32},{40,56},{56,40},{64,80... | collective-permute-start | bytes 786440 | tf_op jit(solution)/shard_map/ppermute | solution.py:18
  343.3 26.5 %collective-permute-start.17 = (bf16[2,64,1024]{1,2,0:T(8,128)(2,1)S(1)}, bf16[2,64,1024]{1,2,0:T(8,128)(2,1)S(1)}, u32[]{:S(2)}, u32[]{:S(2)}) collective-permute-start(bf16[2,64,1024]{1,2,0:T(8,128)(2,1)S(1)} %broadcast_select_fusion.14), channel_id=1, source_target_pairs={{0,32},{32,0},{8,40},{40,8},{16,48},{48,16},{24,56},{56,24},{64,96... | collective-permute-start | bytes 786440 | tf_op jit(solution)/shard_map/ppermute | solution.py:18
  369.9 29.6 %collective-permute-start.18 = (bf16[2,64,1024]{1,2,0:T(8,128)(2,1)S(1)}, bf16[2,64,1024]{1,2,0:T(8,128)(2,1)S(1)}, u32[]{:S(2)}, u32[]{:S(2)}) collective-permute-start(bf16[2,64,1024]{1,2,0:T(8,128)(2,1)S(1)} %get-tuple-element.15), channel_id=1, source_target_pairs={{0,64},{64,0},{8,72},{72,8},{16,80},{80,16},{24,88},{88,24},{32,96... | collective-permute-start | bytes 786440 | tf_op jit(solution)/shard_map/ppermute | solution.py:18
  399.5 14.9 %collective-permute-start.19 = (bf16[2,64,1024]{1,2,0:T(8,128)(2,1)S(1)}, bf16[2,64,1024]{1,2,0:T(8,128)(2,1)S(1)}, u32[]{:S(2)}, u32[]{:S(2)}) collective-permute-start(bf16[2,64,1024]{1,2,0:T(8,128)(2,1)S(1)} %broadcast_select_fusion.26), channel_id=1, source_target_pairs={{0,128},{128,0},{8,136},{136,8},{16,144},{144,16},{24,152},{152,24... | collective-permute-start | bytes 786440 | tf_op jit(solution)/shard_map/ppermute | solution.py:18
  415.4 19.1 %collective-permute-start.20 = (bf16[2,64,1024]{1,2,0:T(8,128)(2,1)S(1)}, bf16[2,64,1024]{1,2,0:T(8,128)(2,1)}, u32[]{:S(2)}, u32[]{:S(2)}) collective-permute-start(bf16[2,64,1024]{1,2,0:T(8,128)(2,1)S(1)} %get-tuple-element.46), channel_id=1, source_target_pairs={{0,8},{8,0},{16,24},{24,16},{32,40},{40,32},{48,56},{56,48},{64,72... | collective-permute-start | bytes 786440 | tf_op jit(solution)/shard_map/ppermute | solution.py:18
  434.5 135.4 %collective-permute-start.21 = (bf16[2,64,1024]{1,2,0:T(8,128)(2,1)}, bf16[2,64,1024]{1,2,0:T(8,128)(2,1)}, u32[]{:S(2)}, u32[]{:S(2)}) collective-permute-start(bf16[2,64,1024]{1,2,0:T(8,128)(2,1)} %collective-permute-done.20), channel_id=1, source_target_pairs={{0,16},{16,0},{8,24},{24,8},{32,48},{48,32},{40,56},{56,40},{64,80... | collective-permute-start | bytes 786440 | tf_op jit(solution)/shard_map/ppermute | solution.py:18
  569.9 16.4 %collective-permute-start.22 = (bf16[2,64,1024]{1,2,0:T(8,128)(2,1)}, bf16[2,64,1024]{1,2,0:T(8,128)(2,1)S(1)}, u32[]{:S(2)}, u32[]{:S(2)}) collective-permute-start(bf16[2,64,1024]{1,2,0:T(8,128)(2,1)} %collective-permute-done.21), channel_id=1, source_target_pairs={{0,32},{32,0},{8,40},{40,8},{16,48},{48,16},{24,56},{56,24},{64,96... | collective-permute-start | bytes 786440 | tf_op jit(solution)/shard_map/ppermute | solution.py:18
  586.3 26.7 %collective-permute-start.23 = (bf16[2,64,1024]{1,2,0:T(8,128)(2,1)S(1)}, bf16[2,64,1024]{1,2,0:T(8,128)(2,1)}, u32[]{:S(2)}, u32[]{:S(2)}) collective-permute-start(bf16[2,64,1024]{1,2,0:T(8,128)(2,1)S(1)} %collective-permute-done.22), channel_id=1, source_target_pairs={{0,64},{64,0},{8,72},{72,8},{16,80},{80,16},{24,88},{88,24},{32,96... | collective-permute-start | bytes 786440 | tf_op jit(solution)/shard_map/ppermute | solution.py:18
  613.1 14.8 %collective-permute-start.24 = (bf16[2,64,1024]{1,2,0:T(8,128)(2,1)}, bf16[2,64,1024]{1,2,0:T(8,128)(2,1)}, u32[]{:S(2)}, u32[]{:S(2)}) collective-permute-start(bf16[2,64,1024]{1,2,0:T(8,128)(2,1)} %collective-permute-done.23), channel_id=1, source_target_pairs={{0,128},{128,0},{8,136},{136,8},{16,144},{144,16},{24,152},{152,24... | collective-permute-start | bytes 786440 | tf_op jit(solution)/shard_map/ppermute | solution.py:18
  (47 other events, 811.9 us)
where the time goes:
time: 642 us; the launch traced here: 631 us
  blocking collectives  240 us (37%)
  waiting for transfers between devices  172 us (27%)
  matrix products  116 us (18%)
  starting transfers between devices  42.3 us (7%)
  other arithmetic  30.1 us (5%)
  local copies, waits for them, and re-layouts  28 us (4%)
    ppermute x20, waiting for transfers between devices, partner(): return lax.ppermute(block, axis, route)  172 us
    unnamed x1, blocking collectives  130 us
    psum x3, blocking collectives, local(): sum_squares = lax.psum(jnp.sum(values * values, axis=2), 'ch')  59.1 us
    dot_general x3, matrix products, local(): jnp.einsum('gtj,tjs->gs', pair_sums, ahead_float, precision=lax.Precision...  53.6 us
    psum x3, blocking collectives, local(): inner = lax.psum(jnp.sum(grad_normed * normed, axis=2), 'ch')  50.8 us
    ppermute x20, starting transfers between devices, partner(): return lax.ppermute(block, axis, route)  29.2 us
    dot_general x3, matrix products, local(): jnp.einsum('tjs,gs->gtj', ahead_hot, taps_local, preferred_element_type=j...  16.9 us
    dot_general x3, matrix products, local(): jnp.einsum('gjt,stgc->sjgc', back_toeplitz, gated_ext, preferred_element_...  15.8 us
  transfers between devices with their start and end apart: 26, of which 15 were waited for; matrix products, arithmetic and copies ran while one was open for 21% of the time, Pallas kernels for 0%

commit v1 on v0

v1 whole, which is shorter than its diff:
```python
import functools

import jax
import jax.numpy as jnp
from jax import lax
from jax.experimental import pallas as pl
from jax.experimental.pallas import tpu as pltpu
from jax.sharding import PartitionSpec as P

GROUP = 16
LAYERS = 3
SEQS = 2
ROWS = 128
LANES = 128
PER = LANES // GROUP
MESH = pl.DeviceIdType.MESH
F32 = jnp.float32
BF16 = jnp.bfloat16


def kernel(
    n, nh, width,
    act, gin, go_hbm, gi_hbm, filt,
    gin_out, ggo_out, ggi_out, gf_out,
    xs, go, gi, vs, vh, ux, zs, g3, gzx, gn, ggo, ggi, g0,
    taps, back, rev, fwdf, bc, bcp, acc, part, lags, fsend, frecv,
    load_sem, hs, hr, bs, br, ps, pr, pr2, fs, fr, as_, ar, ls, lr, out_sem,
):
    chunks = width // LANES
    groups = width // GROUP
    c, h = lax.axis_index("ctx"), lax.axis_index("ch")
    nxt, prv = lax.rem(c + 1, n), lax.rem(c + n - 1, n)
    has_next, has_prev = c < n - 1, c > 0
    zero_i = jnp.int32(0)

    barrier = pltpu.get_barrier_semaphore()

    def greet(cc, hh):
        pl.semaphore_signal(barrier, inc=1, device_id=(cc, hh), device_id_type=MESH)

    for o in range(1, nh):
        greet(c, lax.rem(h + o, nh))

    def greet_ctx(o, carry):
        greet(lax.rem(c + o, n), h)
        return carry

    lax.fori_loop(1, n, greet_ctx, 0)
    for o in range(1, nh):
        greet(nxt, lax.rem(h + o, nh))
        greet(prv, lax.rem(h + o, nh))

    def cols(k):
        return pl.ds(pl.multiple_of(k * LANES, LANES), LANES)

    def load(k, carry):
        pltpu.make_async_copy(act.at[:, :, cols(k)], xs.at[0, k], load_sem.at[0]).start()
        for i in range(LAYERS):
            pltpu.make_async_copy(gi_hbm.at[i, :, :, cols(k)], gi.at[i, k], load_sem.at[1 + i]).start()
        for i in range(LAYERS):
            pltpu.make_async_copy(go_hbm.at[i, :, :, cols(k)], go.at[i, k], load_sem.at[4 + i]).start()
        return carry

    lax.fori_loop(0, chunks, load, 0)

    def wait_bytes(ref, sem):
        pltpu.make_async_copy(ref, ref, sem).wait()

    row = lax.broadcasted_iota(jnp.int32, (ROWS, LANES), 0)
    col = lax.broadcasted_iota(jnp.int32, (ROWS, LANES), 1)
    flip = (row + col == ROWS - 1).astype(BF16)
    group_of = lax.rem(lax.broadcasted_iota(jnp.int32, (ROWS, 2 * LANES), 1), LANES) // GROUP
    group_row = lax.rem(lax.broadcasted_iota(jnp.int32, (1, 2 * LANES), 1), LANES) // GROUP

    for i in range(LAYERS):
        fwdf[i] = filt[i].astype(F32)
        rev[i] = jnp.dot(filt[i], flip, preferred_element_type=F32)

    def build_taps(i):
        def one(g, carry):
            line = jnp.broadcast_to(rev[i, pl.ds(g, 1), :], (ROWS, LANES))
            rolled = pltpu.roll(line, 1, 1, stride=1, stride_axis=0)
            taps[i, g, :, 0:LANES] = jnp.where(col > row, rolled, 0.0).astype(BF16)
            taps[i, g, :, LANES:] = jnp.where(col > row, 0.0, rolled).astype(BF16)
            return carry

        lax.fori_loop(0, groups, one, 0)

    def build_back(i):
        def one(g, carry):
            line = jnp.broadcast_to(fwdf[i, pl.ds(g, 1), :], (ROWS, LANES))
            rolled = pltpu.roll(line, 0, 1, stride=1, stride_axis=0)
            back[i, g, :, 0:LANES] = jnp.where(col < row, 0.0, rolled).astype(BF16)
            back[i, g, :, LANES:] = jnp.where(col < row, rolled, 0.0).astype(BF16)
            return carry

        lax.fori_loop(0, groups, one, 0)

    def halo_fwd(i, k):
        return pltpu.make_async_remote_copy(
            src_ref=vs.at[i, k], dst_ref=vh.at[i, k], send_sem=hs.at[i, k], recv_sem=hr.at[i, k],
            device_id=(nxt, h), device_id_type=MESH)

    def halo_bwd(i, k):
        return pltpu.make_async_remote_copy(
            src_ref=gzx.at[i, k, :, pl.ds(0, ROWS)], dst_ref=gzx.at[i, k, :, pl.ds(ROWS, ROWS)],
            send_sem=bs.at[i, k], recv_sem=br.at[i, k], device_id=(prv, h), device_id_type=MESH)

    def part_own(ph, o):
        return pltpu.make_async_remote_copy(
            src_ref=part.at[ph, h], dst_ref=part.at[ph, h], send_sem=ps.at[ph, o],
            recv_sem=pr.at[ph], device_id=(c, lax.rem(h + o, nh)), device_id_type=MESH)

    def part_next(ph, o):
        return pltpu.make_async_remote_copy(
            src_ref=part.at[ph, h], dst_ref=part.at[ph, nh + h], send_sem=ps.at[ph, nh + o],
            recv_sem=pr2.at[ph], device_id=(nxt, lax.rem(h + o, nh)), device_id_type=MESH)

    def share(ph, to_next):
        for s in range(SEQS):
            part[ph, h, s:s + 1, :] = jnp.sum(acc[s].T, axis=0, keepdims=True)
        for o in range(1, nh):
            part_own(ph, o).start()
        if to_next:
            @pl.when(has_next)
            def _():
                for o in range(nh):
                    part_next(ph, o).start()

    def column(line):
        return jnp.broadcast_to(line, (LANES, ROWS)).T

    def shared(ph, first):
        total = part[ph, first]
        for o in range(1, nh):
            total = total + part[ph, first + o]
        return total

    def wait_own(ph):
        wait_bytes(part.at[ph, pl.ds(0, nh - 1)], pr.at[ph])

    def inverse_of(total):
        return lax.rsqrt(total * (1.0 / (width * nh)) + 1e-06)

    def lag_copy(i, o):
        peer = lax.rem(c + o, n)
        return pltpu.make_async_remote_copy(
            src_ref=fsend.at[i, peer], dst_ref=frecv.at[i, c], send_sem=fs.at[i],
            recv_sem=fr.at[i], device_id=(peer, h), device_id_type=MESH)

    half = ROWS // 2
    def arrive(b):
        block = c if b == 0 else 2 * n - 1 - c
        target = lax.div(block, 2)
        at = pl.multiple_of(lax.rem(block, 2) * half, half)
        return target, pltpu.make_async_remote_copy(
            src_ref=gin.at[:, pl.ds(b * half, half), :], dst_ref=g3.at[:, pl.ds(at, half), :],
            send_sem=as_.at[b], recv_sem=ar.at[lax.rem(block, 2)],
            device_id=(target, h), device_id_type=MESH), pltpu.make_async_copy(
            gin.at[:, pl.ds(b * half, half), :], g3.at[:, pl.ds(at, half), :], ar.at[lax.rem(block, 2)])

    def leave(b, k):
        block = 2 * c + b
        late = lax.div(block, n)
        target = (1 - late) * block + late * (2 * n - 1 - block)
        at = pl.multiple_of(late * half, half)
        src = g0.at[k, :, pl.ds(b * half, half)]
        dst = gin_out.at[:, pl.ds(at, half), cols(k)]
        return target, pltpu.make_async_remote_copy(
            src_ref=src, dst_ref=dst, send_sem=ls.at[b, k], recv_sem=lr.at[late, k],
            device_id=(target, h), device_id_type=MESH), pltpu.make_async_copy(src, dst, lr.at[late, k])

    def both(ref4):
        return jnp.concatenate([ref4[0], ref4[1]], axis=1)

    def grouped(mats, i, k, rhs):
        out = jnp.zeros((ROWS, 2 * LANES), F32)
        for g in range(PER):
            r = jnp.dot(mats[i, k * PER + g], rhs, preferred_element_type=F32)
            out = jnp.where(group_of == g, r, out)
        return out

    build_taps(0)
    wait_bytes(xs.at[0], load_sem.at[0])
    wait_bytes(gi.at[0], load_sem.at[1])
    acc[...] = jnp.zeros_like(acc)

    def prepare(k, carry):
        x = xs[0, k].astype(F32)
        acc[...] += x * x
        vs[0, k] = (gi[0, k].astype(F32) * x).astype(BF16)
        return carry

    lax.fori_loop(0, chunks, prepare, 0)

    pl.semaphore_wait(barrier, n - 1 + 3 * (nh - 1))

    share(0, True)

    @pl.when(has_next)
    def _():
        def send(k, carry):
            halo_fwd(0, k).start()
            return carry

        lax.fori_loop(0, chunks, send, 0)

    for b in range(2):
        target, remote, local = arrive(b)

        @pl.when(target != c)
        def _():
            remote.start()

        @pl.when(target == c)
        def _():
            local.start()

    @pl.when(c == 0)
    def _():
        part[0:LAYERS, nh:] = jnp.zeros((LAYERS, nh, SEQS, ROWS), F32)

        def clear(k, carry):
            for i in range(LAYERS):
                vh[i, k] = jnp.zeros((SEQS, ROWS, LANES), BF16)
            return carry

        lax.fori_loop(0, chunks, clear, 0)

    @pl.when(c == n - 1)
    def _():
        def clear(k, carry):
            for i in range(LAYERS):
                gzx[i, k, :, ROWS:] = jnp.zeros((SEQS, ROWS, LANES), BF16)
            return carry

        lax.fori_loop(0, chunks, clear, 0)

    build_taps(1)
    for i in range(LAYERS):
        wait_bytes(go.at[i], load_sem.at[4 + i])
    for i in range(1, LAYERS):
        wait_bytes(gi.at[i], load_sem.at[1 + i])

    for i in range(LAYERS):
        if i == 1:
            build_taps(2)
        if i == 2:
            build_back(2)
        wait_own(i)

        @pl.when(has_prev)
        def _():
            wait_bytes(part.at[i, pl.ds(nh, nh)], pr2.at[i])

        own = inverse_of(shared(i, 0))
        before = inverse_of(shared(i, nh))
        for s in range(SEQS):
            bc[i, s] = column(own[s:s + 1])
            bcp[s] = column(before[s:s + 1])
        if i + 1 < LAYERS:
            acc[...] = jnp.zeros_like(acc)

        def forward(k, carry):
            @pl.when(has_prev)
            def _():
                halo_fwd(i, k).wait_recv()

            for s in range(SEQS):
                ux[i, k, s, 0:ROWS] = (vh[i, k, s].astype(F32) * bcp[s]).astype(BF16)
                ux[i, k, s, ROWS:] = (
                    gi[i, k, s].astype(F32) * (xs[i, k, s].astype(F32) * bc[i, s])).astype(BF16)
            z = grouped(taps, i, k, both(ux.at[i, k]))
            for s in range(SEQS):
                zs_part = z[:, s * LANES:(s + 1) * LANES]
                zs[i, k, s] = zs_part
                if i + 1 < LAYERS:
                    x_next = (go[i, k, s].astype(F32) * zs_part).astype(BF16)
                    xs[i + 1, k, s] = x_next
                    x_wide = x_next.astype(F32)
                    acc[s] += x_wide * x_wide
                    vs[i + 1, k, s] = (gi[i + 1, k, s].astype(F32) * x_wide).astype(BF16)
            if i + 1 < LAYERS:
                @pl.when(has_next)
                def _():
                    halo_fwd(i + 1, k).start()
            return carry

        lax.fori_loop(0, chunks, forward, 0)
        if i + 1 < LAYERS:
            share(i + 1, True)

    for b in range(2):
        wait_bytes(g3.at[:, pl.ds(b * half, half), :], ar.at[b])

    for i in reversed(range(LAYERS)):
        ph = LAYERS + i
        last = i == LAYERS - 1
        if not last:
            wait_own(LAYERS + i + 1)
            mean = shared(LAYERS + i + 1, 0) * (1.0 / (width * nh))
            for s in range(SEQS):
                bcp[s] = column(mean[s:s + 1]) * bc[i + 1, s]

        def enter(k, carry):
            for s in range(SEQS):
                if last:
                    g = g3[s, :, cols(k)].astype(F32)
                else:
                    g = (bc[i + 1, s] * (gn[k, s] - xs[i + 1, k, s].astype(F32) * bcp[s])).astype(BF16).astype(F32)
                gzx[i, k, s, 0:ROWS] = (go[i, k, s].astype(F32) * g).astype(BF16)
                ggo[i, k, s] = (g * zs[i, k, s]).astype(BF16)

            @pl.when(has_prev)
            def _():
                halo_bwd(i, k).start()

            pltpu.make_async_copy(ggo.at[i, k], ggo_out.at[i, :, :, cols(k)], out_sem.at[i]).start()
            return carry

        lax.fori_loop(0, chunks, enter, 0)

        if last:
            build_back(1)
            build_back(0)

        def diagonals(k, carry):
            grad = jnp.concatenate([gzx[i, k, 0, 0:ROWS], gzx[i, k, 1, 0:ROWS]], axis=1)
            turned = jnp.dot(flip, grad, preferred_element_type=F32)
            rhs = both(ux.at[i, k])
            for g in range(PER):
                lhs = jnp.where(group_row == g, turned, 0.0).astype(BF16)
                prod = lax.dot_general(lhs, rhs, (((1,), (1,)), ((), ())), preferred_element_type=F32)
                merged = jnp.where(row + col > ROWS - 1, prod[:, 0:LANES], prod[:, LANES:])
                rolled = pltpu.roll(merged, 1, 1, stride=1, stride_axis=0)
                lags[pl.ds(k * PER + g, 1), :] = jnp.sum(rolled, axis=0, keepdims=True)
            return carry

        lax.fori_loop(0, chunks, diagonals, 0)
        per = ROWS // n
        peer_row = lax.broadcasted_iota(jnp.int32, (n, LANES), 0)
        peer_col = lax.broadcasted_iota(jnp.int32, (n, LANES), 1)
        pieces = []
        for q in range(per):
            pick = (lax.rem(peer_col + peer_row * per + q, ROWS) == 0).astype(F32)
            pieces.append(lax.dot_general(
                pick, lags[...], (((1,), (1,)), ((), ())), preferred_element_type=F32,
                precision=lax.Precision.HIGHEST))
        lines = jnp.concatenate(pieces, axis=1)
        span = lines.shape[1] // 2
        for p in range(n):
            for r in range(2):
                fsend[i, p, r:r + 1, :] = lines[p:p + 1, r * span:(r + 1) * span]
        frecv[i, c] = fsend[i, c]

        def send_lags(o, carry):
            lag_copy(i, o).start()
            return carry

        lax.fori_loop(1, n, send_lags, 0)

        acc[...] = jnp.zeros_like(acc)

        def backward(k, carry):
            @pl.when(has_next)
            def _():
                halo_bwd(i, k).wait_recv()

            gu = grouped(back, i, k, both(gzx.at[i, k]))
            for s in range(SEQS):
                gu_part = gu[:, s * LANES:(s + 1) * LANES]
                normed = xs[i, k, s].astype(F32) * bc[i, s]
                ggi[i, k, s] = (gu_part * normed).astype(BF16)
                gn_part = gu_part * gi[i, k, s].astype(F32)
                gn[k, s] = gn_part
                acc[s] += gn_part * normed
            pltpu.make_async_copy(ggi.at[i, k], ggi_out.at[i, :, :, cols(k)], out_sem.at[LAYERS + i]).start()
            return carry

        lax.fori_loop(0, chunks, backward, 0)
        share(ph, False)

    wait_own(LAYERS)
    mean = shared(LAYERS, 0) * (1.0 / (width * nh))
    for s in range(SEQS):
        bcp[s] = column(mean[s:s + 1]) * bc[0, s]

    def finish(k, carry):
        for s in range(SEQS):
            g0[k, s] = (bc[0, s] * (gn[k, s] - xs[0, k, s].astype(F32) * bcp[s])).astype(BF16)
        for b in range(2):
            target, remote, local = leave(b, k)

            @pl.when(target != c)
            def _():
                remote.start()

            @pl.when(target == c)
            def _():
                local.start()
        return carry

    lax.fori_loop(0, chunks, finish, 0)

    for i in range(LAYERS):
        wait_bytes(frecv.at[i, pl.ds(0, n - 1)], fr.at[i])
        gf_out[i] = jnp.sum(frecv[i], axis=0)

    for i in range(LAYERS):
        wait_bytes(ggo.at[i], out_sem.at[i])
        wait_bytes(ggi.at[i], out_sem.at[LAYERS + i])
        wait_bytes(fsend.at[i, pl.ds(0, n - 1)], fs.at[i])
    for ph in range(2 * LAYERS):
        for o in range(1, nh):
            part_own(ph, o).wait_send()
    for b in range(2):
        target, remote, local = arrive(b)

        @pl.when(target != c)
        def _():
            remote.wait_send()

    @pl.when(has_next)
    def _():
        for ph in range(LAYERS):
            for o in range(nh):
                part_next(ph, o).wait_send()

        def drain(k, carry):
            for i in range(LAYERS):
                halo_fwd(i, k).wait_send()
            return carry

        lax.fori_loop(0, chunks, drain, 0)

    @pl.when(has_prev)
    def _():
        def drain(k, carry):
            for i in range(LAYERS):
                halo_bwd(i, k).wait_send()
            return carry

        lax.fori_loop(0, chunks, drain, 0)

    def drain(k, carry):
        for b in range(2):
            target, remote, local = leave(b, k)

            @pl.when(target != c)
            def _():
                remote.wait_send()

            wait_bytes(gin_out.at[:, pl.ds(b * half, half), cols(k)], lr.at[b, k])
        return carry

    lax.fori_loop(0, chunks, drain, 0)


def local(n, nh, activations, grad_in, gate_out, gate_in, filters):
    width = activations.shape[2]
    chunks, groups = width // LANES, width // GROUP
    per = ROWS // n
    span = per * groups // 2
    block = (SEQS, ROWS, LANES)
    wide = (SEQS, 2 * ROWS, LANES)
    any_spec = pl.BlockSpec(memory_space=pl.ANY)
    vmem_spec = pl.BlockSpec(memory_space=pltpu.VMEM)
    dma = pltpu.SemaphoreType.DMA
    grad_input, ggo, ggi, lags = pl.pallas_call(
        functools.partial(kernel, n, nh, width),
        out_shape=(
            jax.ShapeDtypeStruct(activations.shape, BF16),
            jax.ShapeDtypeStruct(gate_out.shape, BF16),
            jax.ShapeDtypeStruct(gate_in.shape, BF16),
            jax.ShapeDtypeStruct((LAYERS, 2, span), F32),
        ),
        in_specs=[any_spec] * 4 + [vmem_spec],
        out_specs=(any_spec, any_spec, any_spec, vmem_spec),
        scratch_shapes=[
            pltpu.VMEM((LAYERS, chunks) + block, BF16),
            pltpu.VMEM((LAYERS, chunks) + block, BF16),
            pltpu.VMEM((LAYERS, chunks) + block, BF16),
            pltpu.VMEM((LAYERS, chunks) + block, BF16),
            pltpu.VMEM((LAYERS, chunks) + block, BF16),
            pltpu.VMEM((LAYERS, chunks) + wide, BF16),
            pltpu.VMEM((LAYERS, chunks) + block, F32),
            pltpu.VMEM((SEQS, ROWS, width), BF16),
            pltpu.VMEM((LAYERS, chunks) + wide, BF16),
            pltpu.VMEM((chunks,) + block, F32),
            pltpu.VMEM((LAYERS, chunks) + block, BF16),
            pltpu.VMEM((LAYERS, chunks) + block, BF16),
            pltpu.VMEM((chunks,) + block, BF16),
            pltpu.VMEM((LAYERS, groups, ROWS, 2 * LANES), BF16),
            pltpu.VMEM((LAYERS, groups, ROWS, 2 * LANES), BF16),
            pltpu.VMEM((LAYERS, groups, LANES), F32),
            pltpu.VMEM((LAYERS, groups, LANES), F32),
            pltpu.VMEM((LAYERS,) + block, F32),
            pltpu.VMEM(block, F32),
            pltpu.VMEM(block, F32),
            pltpu.VMEM((2 * LAYERS, 2 * nh, SEQS, ROWS), F32),
            pltpu.VMEM((groups, LANES), F32),
            pltpu.VMEM((LAYERS, n, 2, span), F32),
            pltpu.VMEM((LAYERS, n, 2, span), F32),
            dma((7,)),
            dma((LAYERS, chunks)), dma((LAYERS, chunks)),
            dma((LAYERS, chunks)), dma((LAYERS, chunks)),
            dma((2 * LAYERS, 2 * nh)), dma((2 * LAYERS,)), dma((2 * LAYERS,)),
            dma((LAYERS,)), dma((LAYERS,)),
            dma((2,)), dma((2,)),
            dma((2, chunks)), dma((2, chunks)),
            dma((2 * LAYERS,)),
        ],
        compiler_params=pltpu.CompilerParams(
            collective_id=0, has_side_effects=True, vmem_limit_bytes=64 * 1024 * 1024 - 65536),
    )(activations, grad_in, gate_out, gate_in, filters)
    grad_filters = lags.reshape(LAYERS, per, groups).transpose(0, 2, 1)
    return grad_input, ggo, ggi, grad_filters


def solution(mesh):
    n, nh = mesh.shape["ctx"], mesh.shape["ch"]
    return jax.shard_map(
        functools.partial(local, n, nh),
        mesh=mesh,
        in_specs=(
            P(None, "ctx", "ch"),
            P(None, "ctx", "ch"),
            P(None, None, "ctx", "ch"),
            P(None, None, "ctx", "ch"),
            P(None, "ch", None),
        ),
        out_specs=(
            P(None, "ctx", "ch"),
            P(None, None, "ctx", "ch"),
            P(None, None, "ctx", "ch"),
            P(None, "ch", "ctx"),
        ),
        check_vma=False,
    )
```

time: 642 us -> 139 us (0.22); the launches traced: 631 us -> 139 us
  blocking collectives: 240 us -> 0 us
  waiting for transfers between devices: 172 us -> 0 us
  Pallas kernels: 0 us -> 131 us
  matrix products: 116 us -> 0 us
  starting transfers between devices: 42.3 us -> 0 us
  other arithmetic: 30.1 us -> 0 us
  local copies, waits for them, and re-layouts: 28 us -> 7.24 us
    ppermute x26 -> x0, waiting for transfers between devices: 172 us -> none  [the longest x20 172 us: partner(): return lax.ppermute(block, axis, route)]
    pallas_call x0 -> x1, Pallas kernels: none -> 131 us  [local(): pl.pallas_call(functools.partial(kernel, n, nh, width), out_shape=(jax.Sh...]
    unnamed x1 -> x0, blocking collectives: 130 us -> none
    dot_general x18 -> x0, matrix products: 116 us -> none  [the longest x3 53.6 us: local(): jnp.einsum('gtj,tjs->gs', pair_sums, ahead_float, precision=lax.Precision...]
    psum x6 -> x0, blocking collectives: 110 us -> none  [the longest x3 59.1 us: local(): sum_squares = lax.psum(jnp.sum(values * values, axis=2), 'ch')]
    ppermute x26 -> x0, starting transfers between devices: 42.3 us -> none  [the longest x20 29.2 us: partner(): return lax.ppermute(block, axis, route)]
    convert_element_type x10 -> x0, other arithmetic: 10.9 us -> none  [the longest x3 4.13 us: local(): in_grads[layer_index] = (spread_back * normed).astype(jnp.bfloat16)]
    select_n x12 -> x0, other arithmetic: 10.7 us -> none  [the longest x5 7.46 us: arrive_paired(): outgoing = jnp.where(lower, trailing, leading)]
  transfers between devices with their start and end apart: 26 -> 0, of which waited for: 15 -> 0; matrix products, arithmetic and copies ran while one was open for 21% -> 0% of each run, Pallas kernels for 0% -> 0%
where the time goes in v1:
time: 139 us
  Pallas kernels  131 us (94%)
  local copies, waits for them, and re-layouts  7.24 us (5%)
    pallas_call x1, Pallas kernels, local(): pl.pallas_call(functools.partial(kernel, n, nh, width), out_shape=(jax.Sh...  131 us
    unnamed x5, local copies, waits for them, and re-layouts  5.89 us

profile of v1, /device:TPU:16, one launch (start us, length us, event | category | flops | bytes accessed | tf_op | source)
XLA Modules:
  0.0 139.1 jit_solution(17132017028688462633)
XLA Ops:
  0.6 131.2 %shard_map.84 = (bf16[2,128,1024]{2,1,0:T(8,128)(2,1)}, bf16[3,2,128,1024]{3,2,1,0:T(8,128)(2,1)}, bf16[3,2,128,1024]{3,2,1,0:T(8,128)(2,1)}, f32[3,2,128]{2,1,0:T(2,128)}) custom-call(bf16[2,128,1024]{2,1,0:T(8,128)(2,1)} %act.1, bf16[2,128,1024]{2,1,0:T(8,128)(2,1)} %gin.1, bf16[3,2,128,1024]{3,2,1,0:T(8,128)(2,1)} %go_hbm.1, ...), custom_call_target="tpu_custom_call" | custom-call | tf_op jit(solution)/shard_map/pallas_call | solution.py:469
  131.8 1.4 reshape.11
  133.2 1.9 %copy.12 = bf16[2,128,1024]{2,1,0:T(8,128)(2,1)} copy(bf16[2,128,1024]{2,1,0:T(8,128)(2,1)} %get-tuple-element.16) | data formatting | bytes 1048576
  135.1 0.0 copy-start
  135.1 2.9 %copy.13 = bf16[3,2,128,1024]{3,2,1,0:T(8,128)(2,1)} copy(bf16[3,2,128,1024]{3,2,1,0:T(8,128)(2,1)} %get-tuple-element.17) | data formatting | bytes 3145728
  137.9 0.0 copy-done
  137.9 1.1 copy.14
Async XLA Ops:
  135.1 2.9 %copy-start = (bf16[3,2,128,1024]{3,2,1,0:T(8,128)(2,1)S(1)}, bf16[3,2,128,1024]{3,2,1,0:T(8,128)(2,1)}, u32[]{:S(2)}) copy-start(bf16[3,2,128,1024]{3,2,1,0:T(8,128)(2,1)} %get-tuple-element.18) | copy-start | bytes 4718596

commit v2 on v1

--- a/solution.py
+++ b/solution.py
@@ -70,31 +70,37 @@
     col = lax.broadcasted_iota(jnp.int32, (ROWS, LANES), 1)
     flip = (row + col == ROWS - 1).astype(BF16)
     group_of = lax.rem(lax.broadcasted_iota(jnp.int32, (ROWS, 2 * LANES), 1), LANES) // GROUP
-    group_row = lax.rem(lax.broadcasted_iota(jnp.int32, (1, 2 * LANES), 1), LANES) // GROUP
+    tiles = ROWS // 16
+    own_group = (lax.broadcasted_iota(jnp.int32, (ROWS, 2 * LANES), 0) // 16 == group_of).astype(BF16)
 
     for i in range(LAYERS):
         fwdf[i] = filt[i].astype(F32)
         rev[i] = jnp.dot(filt[i], flip, preferred_element_type=F32)
 
+    above = (col > row).astype(BF16)
+    not_below = (col >= row).astype(BF16)
+
+    def circulant(mats, i, lines, shift, first):
+        def some(q, carry):
+            for r in range(PER):
+                g = q * PER + r
+                line = jnp.broadcast_to(lines[i, pl.ds(g, 1), :], (16, LANES))
+                base = pltpu.roll(line, shift, 1, stride=1, stride_axis=0)
+                for t in range(ROWS // 16):
+                    at = slice(16 * t, 16 * t + 16)
+                    turn = (pltpu.roll(base, 16 * t, 1) if t else base).astype(BF16)
+                    kept = turn * first[at]
+                    mats[i, g, at, 0:LANES] = kept
+                    mats[i, g, at, LANES:] = turn - kept
+            return carry
+
+        lax.fori_loop(0, chunks, some, 0)
+
     def build_taps(i):
-        def one(g, carry):
-            line = jnp.broadcast_to(rev[i, pl.ds(g, 1), :], (ROWS, LANES))
-            rolled = pltpu.roll(line, 1, 1, stride=1, stride_axis=0)
-            taps[i, g, :, 0:LANES] = jnp.where(col > row, rolled, 0.0).astype(BF16)
-            taps[i, g, :, LANES:] = jnp.where(col > row, 0.0, rolled).astype(BF16)
-            return carry
-
-        lax.fori_loop(0, groups, one, 0)
+        circulant(taps, i, rev, 1, above)
 
     def build_back(i):
-        def one(g, carry):
-            line = jnp.broadcast_to(fwdf[i, pl.ds(g, 1), :], (ROWS, LANES))
-            rolled = pltpu.roll(line, 0, 1, stride=1, stride_axis=0)
-            back[i, g, :, 0:LANES] = jnp.where(col < row, 0.0, rolled).astype(BF16)
-            back[i, g, :, LANES:] = jnp.where(col < row, rolled, 0.0).astype(BF16)
-            return carry
-
-        lax.fori_loop(0, groups, one, 0)
+        circulant(back, i, fwdf, 0, not_below)
 
     def halo_fwd(i, k):
         return pltpu.make_async_remote_copy(
@@ -149,15 +155,16 @@
             recv_sem=fr.at[i], device_id=(peer, h), device_id_type=MESH)
 
     half = ROWS // 2
-    def arrive(b):
+    def arrive(b, k):
         block = c if b == 0 else 2 * n - 1 - c
         target = lax.div(block, 2)
-        at = pl.multiple_of(lax.rem(block, 2) * half, half)
+        slot = lax.rem(block, 2)
+        at = pl.multiple_of(slot * half, half)
+        src = gin.at[:, pl.ds(b * half, half), cols(k)]
+        dst = g3.at[:, pl.ds(at, half), cols(k)]
         return target, pltpu.make_async_remote_copy(
-            src_ref=gin.at[:, pl.ds(b * half, half), :], dst_ref=g3.at[:, pl.ds(at, half), :],
-            send_sem=as_.at[b], recv_sem=ar.at[lax.rem(block, 2)],
-            device_id=(target, h), device_id_type=MESH), pltpu.make_async_copy(
-            gin.at[:, pl.ds(b * half, half), :], g3.at[:, pl.ds(at, half), :], ar.at[lax.rem(block, 2)])
+            src_ref=src, dst_ref=dst, send_sem=as_.at[b, k], recv_sem=ar.at[slot, k],
+            device_id=(target, h), device_id_type=MESH), pltpu.make_async_copy(src, dst, ar.at[slot, k])
 
     def leave(b, k):
         block = 2 * c + b
@@ -204,17 +211,6 @@
             return carry
 
         lax.fori_loop(0, chunks, send, 0)
-
-    for b in range(2):
-        target, remote, local = arrive(b)
-
-        @pl.when(target != c)
-        def _():
-            remote.start()
-
-        @pl.when(target == c)
-        def _():
-            local.start()
 
     @pl.when(c == 0)
     def _():
@@ -284,15 +280,23 @@
                 @pl.when(has_next)
                 def _():
                     halo_fwd(i + 1, k).start()
+
+                target, remote, local = arrive(i, k)
+
+                @pl.when(target != c)
+                def _():
+                    remote.start()
+
+                @pl.when(target == c)
+                def _():
+                    local.start()
             return carry
 
         lax.fori_loop(0, chunks, forward, 0)
         if i + 1 < LAYERS:
             share(i + 1, True)
 
-    for b in range(2):
-        wait_bytes(g3.at[:, pl.ds(b * half, half), :], ar.at[b])
-
+    early = chunks // 2
     for i in reversed(range(LAYERS)):
         ph = LAYERS + i
         last = i == LAYERS - 1
@@ -303,6 +307,9 @@
                 bcp[s] = column(mean[s:s + 1]) * bc[i + 1, s]
 
         def enter(k, carry):
+            if last:
+                for b in range(2):
+                    wait_bytes(g3.at[:, pl.ds(b * half, half), cols(k)], ar.at[b, k])
             for s in range(SEQS):
                 if last:
                     g = g3[s, :, cols(k)].astype(F32)
@@ -326,17 +333,45 @@
 
         def diagonals(k, carry):
             grad = jnp.concatenate([gzx[i, k, 0, 0:ROWS], gzx[i, k, 1, 0:ROWS]], axis=1)
-            turned = jnp.dot(flip, grad, preferred_element_type=F32)
-            rhs = both(ux.at[i, k])
+            turned = jnp.dot(flip, grad, preferred_element_type=F32).astype(BF16)
+            rows = both(ux.at[i, k])
+            lhs, rhs = [], []
+            for t in range(tiles):
+                tile = turned[ROWS - 16 * t - 16:ROWS - 16 * t]
+                lhs.append(jnp.concatenate([tile] * PER, axis=0) * own_group)
+                rhs.append(rows[16 * t:16 * t + ROWS + 16])
+            prod = lax.dot_general(
+                jnp.concatenate(lhs, axis=1), jnp.concatenate(rhs, axis=1),
+                (((1,), (1,)), ((), ())), preferred_element_type=F32)
+            tail = jnp.concatenate([prod[:, ROWS:], jnp.zeros((ROWS, LANES - 16), F32)], axis=1)
+            merged = jnp.where(col + lax.rem(row, 16) > 15, prod[:, 0:LANES], tail)
             for g in range(PER):
-                lhs = jnp.where(group_row == g, turned, 0.0).astype(BF16)
-                prod = lax.dot_general(lhs, rhs, (((1,), (1,)), ((), ())), preferred_element_type=F32)
-                merged = jnp.where(row + col > ROWS - 1, prod[:, 0:LANES], prod[:, LANES:])
-                rolled = pltpu.roll(merged, 1, 1, stride=1, stride_axis=0)
+                rolled = pltpu.roll(merged[16 * g:16 * g + 16], LANES - 15, 1, stride=1, stride_axis=0)
                 lags[pl.ds(k * PER + g, 1), :] = jnp.sum(rolled, axis=0, keepdims=True)
             return carry
 
-        lax.fori_loop(0, chunks, diagonals, 0)
+        lax.fori_loop(0, early, diagonals, 0)
+        acc[...] = jnp.zeros_like(acc)
+
+        def backward(k, carry):
+            @pl.when(has_next)
+            def _():
+                halo_bwd(i, k).wait_recv()
+
+            gu = grouped(back, i, k, both(gzx.at[i, k]))
+            for s in range(SEQS):
+                gu_part = gu[:, s * LANES:(s + 1) * LANES]
+                normed = xs[i, k, s].astype(F32) * bc[i, s]
+                ggi[i, k, s] = (gu_part * normed).astype(BF16)
+                gn_part = gu_part * gi[i, k, s].astype(F32)
+                gn[k, s] = gn_part
+                acc[s] += gn_part * normed
+            pltpu.make_async_copy(ggi.at[i, k], ggi_out.at[i, :, :, cols(k)], out_sem.at[LAYERS + i]).start()
+            return carry
+
+        lax.fori_loop(0, chunks, backward, 0)
+        share(ph, False)
+        lax.fori_loop(early, chunks, diagonals, 0)
         per = ROWS // n
         peer_row = lax.broadcasted_iota(jnp.int32, (n, LANES), 0)
         peer_col = lax.broadcasted_iota(jnp.int32, (n, LANES), 1)
@@ -359,27 +394,6 @@
 
         lax.fori_loop(1, n, send_lags, 0)
 
-        acc[...] = jnp.zeros_like(acc)
-
-        def backward(k, carry):
-            @pl.when(has_next)
-            def _():
-                halo_bwd(i, k).wait_recv()
-
-            gu = grouped(back, i, k, both(gzx.at[i, k]))
-            for s in range(SEQS):
-                gu_part = gu[:, s * LANES:(s + 1) * LANES]
-                normed = xs[i, k, s].astype(F32) * bc[i, s]
-                ggi[i, k, s] = (gu_part * normed).astype(BF16)
-                gn_part = gu_part * gi[i, k, s].astype(F32)
-                gn[k, s] = gn_part
-                acc[s] += gn_part * normed
-            pltpu.make_async_copy(ggi.at[i, k], ggi_out.at[i, :, :, cols(k)], out_sem.at[LAYERS + i]).start()
-            return carry
-
-        lax.fori_loop(0, chunks, backward, 0)
-        share(ph, False)
-
     wait_own(LAYERS)
     mean = shared(LAYERS, 0) * (1.0 / (width * nh))
     for s in range(SEQS):
@@ -413,13 +427,6 @@
     for ph in range(2 * LAYERS):
         for o in range(1, nh):
             part_own(ph, o).wait_send()
-    for b in range(2):
-        target, remote, local = arrive(b)
-
-        @pl.when(target != c)
-        def _():
-            remote.wait_send()
-
     @pl.when(has_next)
     def _():
         for ph in range(LAYERS):
@@ -444,16 +451,32 @@
 
     def drain(k, carry):
         for b in range(2):
-            target, remote, local = leave(b, k)
-
-            @pl.when(target != c)
-            def _():
-                remote.wait_send()
+            for target, remote, local in (leave(b, k), arrive(b, k)):
+                @pl.when(target != c)
+                def _():
+                    remote.wait_send()
 
             wait_bytes(gin_out.at[:, pl.ds(b * half, half), cols(k)], lr.at[b, k])
         return carry
 
     lax.fori_loop(0, chunks, drain, 0)
+
+
+def hand_over(per, groups, a, b, c, d, a_out, b_out, c_out, d_out, held, get, put):
+    pairs = [(a, a_out)] + [(b.at[i], b_out.at[i]) for i in range(LAYERS)]
+    pairs += [(c.at[i], c_out.at[i]) for i in range(LAYERS)]
+    for j, (src, _) in enumerate(pairs):
+        pltpu.make_async_copy(src, held.at[j], get.at[j]).start()
+    half = per // 2
+    for i in range(LAYERS):
+        for q in range(per):
+            at = (q % half) * groups
+            d_out[i, q:q + 1, :] = d[i, q // half:q // half + 1, at:at + groups]
+    for j, (src, dst) in enumerate(pairs):
+        pltpu.make_async_copy(src, held.at[j], get.at[j]).wait()
+        pltpu.make_async_copy(held.at[j], dst, put.at[j]).start()
+    for j, (src, dst) in enumerate(pairs):
+        pltpu.make_async_copy(held.at[j], dst, put.at[j]).wait()
 
 
 def local(n, nh, activations, grad_in, gate_out, gate_in, filters):
@@ -506,15 +529,29 @@
             dma((LAYERS, chunks)), dma((LAYERS, chunks)),
             dma((2 * LAYERS, 2 * nh)), dma((2 * LAYERS,)), dma((2 * LAYERS,)),
             dma((LAYERS,)), dma((LAYERS,)),
-            dma((2,)), dma((2,)),
+            dma((2, chunks)), dma((2, chunks)),
             dma((2, chunks)), dma((2, chunks)),
             dma((2 * LAYERS,)),
         ],
         compiler_params=pltpu.CompilerParams(
             collective_id=0, has_side_effects=True, vmem_limit_bytes=64 * 1024 * 1024 - 65536),
     )(activations, grad_in, gate_out, gate_in, filters)
-    grad_filters = lags.reshape(LAYERS, per, groups).transpose(0, 2, 1)
-    return grad_input, ggo, ggi, grad_filters
+    grad_input, ggo, ggi, grad_filters = pl.pallas_call(
+        functools.partial(hand_over, per, groups),
+        out_shape=(
+            jax.ShapeDtypeStruct(activations.shape, BF16),
+            jax.ShapeDtypeStruct(gate_out.shape, BF16),
+            jax.ShapeDtypeStruct(gate_in.shape, BF16),
+            jax.ShapeDtypeStruct((LAYERS, per, groups), F32),
+        ),
+        in_specs=[any_spec] * 3 + [vmem_spec],
+        out_specs=(any_spec, any_spec, any_spec, vmem_spec),
+        scratch_shapes=[
+            pltpu.VMEM((2 * LAYERS + 1,) + activations.shape, BF16),
+            dma((2 * LAYERS + 1,)), dma((2 * LAYERS + 1,)),
+        ],
+    )(grad_input, ggo, ggi, lags)
+    return grad_input, ggo, ggi, grad_filters.transpose(0, 2, 1)
 
 
 def solution(mesh):

time: 139 us -> 118 us (0.85)
  Pallas kernels: 131 us -> 116 us
  local copies, waits for them, and re-layouts: 7.24 us -> 0 us
    pallas_call x1, Pallas kernels: 131 us -> 112 us  [local(): pl.pallas_call(functools.partial(kernel, n, nh, width), out_shape=(jax.Sh...]
    unnamed x5 -> x0, local copies, waits for them, and re-layouts: 5.89 us -> none
    pallas_call x0 -> x1, Pallas kernels: none -> 4.3 us  [local(): pl.pallas_call(functools.partial(hand_over, per, groups), out_shape=(jax....]
where the time goes in v2:
time: 118 us; the launch traced here: 117 us
  Pallas kernels  116 us (98%)
    pallas_call x1, Pallas kernels, local(): pl.pallas_call(functools.partial(kernel, n, nh, width), out_shape=(jax.Sh...  112 us
    pallas_call x1, Pallas kernels, local(): pl.pallas_call(functools.partial(hand_over, per, groups), out_shape=(jax....  4.3 us

profile of v2, /device:TPU:16, one launch (start us, length us, event | category | flops | bytes accessed | tf_op | source)
XLA Modules:
  0.0 116.9 jit_solution(17791857446690153439)
XLA Ops:
  0.6 112.0 %shard_map.84 = (bf16[2,128,1024]{2,1,0:T(8,128)(2,1)}, bf16[3,2,128,1024]{3,2,1,0:T(8,128)(2,1)}, bf16[3,2,128,1024]{3,2,1,0:T(8,128)(2,1)}, f32[3,2,128]{2,1,0:T(2,128)}) custom-call(bf16[2,128,1024]{2,1,0:T(8,128)(2,1)} %act.1, bf16[2,128,1024]{2,1,0:T(8,128)(2,1)} %gin.1, bf16[3,2,128,1024]{3,2,1,0:T(8,128)(2,1)} %go_hbm.1, ...), custom_call_target="tpu_custom_call" | custom-call | tf_op jit(solution)/shard_map/pallas_call | solution.py:492
  112.6 4.3 %shard_map.85 = (bf16[2,128,1024]{2,1,0:T(8,128)(2,1)}, bf16[3,2,128,1024]{3,2,1,0:T(8,128)(2,1)}, bf16[3,2,128,1024]{3,2,1,0:T(8,128)(2,1)}, f32[3,4,64]{2,1,0:T(4,128)}) custom-call(bf16[2,128,1024]{2,1,0:T(8,128)(2,1)} %get-tuple-element.12.a, bf16[3,2,128,1024]{3,2,1,0:T(8,128)(2,1)} %get-tuple-element.13.b, ...), custom_call_target="tpu_custom_call" | custom-call | tf_op jit(solution)/shard_map/pallas_call | solution.py:539

commit v3 on v2

--- a/solution.py
+++ b/solution.py
@@ -14,6 +14,7 @@
 LANES = 128
 PER = LANES // GROUP
 MESH = pl.DeviceIdType.MESH
+ARRIVE = (1, 2)
 F32 = jnp.float32
 BF16 = jnp.bfloat16
 
@@ -22,9 +23,9 @@
     n, nh, width,
     act, gin, go_hbm, gi_hbm, filt,
     gin_out, ggo_out, ggi_out, gf_out,
-    xs, go, gi, vs, vh, ux, zs, g3, gzx, gn, ggo, ggi, g0,
+    xs, go, gi, vs, vh, ux, zs, g3, relay, gzx, gn, ggo, ggi, g0,
     taps, back, rev, fwdf, bc, bcp, acc, part, lags, fsend, frecv,
-    load_sem, hs, hr, bs, br, ps, pr, pr2, fs, fr, as_, ar, ls, lr, out_sem,
+    load_sem, hs, hr, bs, br, ps, pr, pr2, fs, fr, as_, ar, sw, ls, lr, out_sem,
 ):
     chunks = width // LANES
     groups = width // GROUP
@@ -155,16 +156,48 @@
             recv_sem=fr.at[i], device_id=(peer, h), device_id_type=MESH)
 
     half = ROWS // 2
+    side = lax.div(c, lax.div(n, 2))
+    near = c - side * lax.div(n, 2)
+    chip = lax.div(near, 2)
+    trade = (3 * n // 8 if n == 32 else 0) * (
+        lax.div(7 - chip, 7) - lax.div(36 - (chip - 6) * (chip - 6), 36))
+    give_to = (1 - side) * (c + lax.div(n, 2)) + side * (near + trade)
+    across = (1 - side) * (c + trade + lax.div(n, 2)) + side * near
+
+    def swap():
+        return pltpu.make_async_remote_copy(
+            src_ref=gin.at[:, pl.ds(pl.multiple_of((1 - side) * half, half), half), :], dst_ref=relay,
+            send_sem=sw.at[0], recv_sem=sw.at[1], device_id=(give_to, h), device_id_type=MESH)
+
     def arrive(b, k):
-        block = c if b == 0 else 2 * n - 1 - c
+        source = c if b == 0 else across
+        block = source + side * (2 * n - 1 - 2 * source)
         target = lax.div(block, 2)
         slot = lax.rem(block, 2)
         at = pl.multiple_of(slot * half, half)
-        src = gin.at[:, pl.ds(b * half, half), cols(k)]
+        src = gin.at[:, pl.ds(pl.multiple_of(side * half, half), half), cols(k)] if b == 0 else relay.at[:, :, cols(k)]
         dst = g3.at[:, pl.ds(at, half), cols(k)]
         return target, pltpu.make_async_remote_copy(
             src_ref=src, dst_ref=dst, send_sem=as_.at[b, k], recv_sem=ar.at[slot, k],
             device_id=(target, h), device_id_type=MESH), pltpu.make_async_copy(src, dst, ar.at[slot, k])
+
+    def send_arrive(b):
+        if b == 1:
+            swap().wait_recv()
+
+        def some(k, carry):
+            target, remote, local = arrive(b, k)
+
+            @pl.when(target != c)
+            def _():
+                remote.start()
+
+            @pl.when(target == c)
+            def _():
+                local.start()
+            return carry
+
+        lax.fori_loop(0, chunks, some, 0)
 
     def leave(b, k):
         block = 2 * c + b
@@ -232,12 +265,16 @@
 
         lax.fori_loop(0, chunks, clear, 0)
 
+    swap().start()
+    if 0 in ARRIVE:
+        send_arrive(ARRIVE.index(0))
     build_taps(1)
     for i in range(LAYERS):
         wait_bytes(go.at[i], load_sem.at[4 + i])
     for i in range(1, LAYERS):
         wait_bytes(gi.at[i], load_sem.at[1 + i])
 
+    step = 2 if chunks % 2 == 0 else 1
     for i in range(LAYERS):
         if i == 1:
             build_taps(2)
@@ -257,11 +294,7 @@
         if i + 1 < LAYERS:
             acc[...] = jnp.zeros_like(acc)
 
-        def forward(k, carry):
-            @pl.when(has_prev)
-            def _():
-                halo_fwd(i, k).wait_recv()
-
+        def forward_one(k):
             for s in range(SEQS):
                 ux[i, k, s, 0:ROWS] = (vh[i, k, s].astype(F32) * bcp[s]).astype(BF16)
                 ux[i, k, s, ROWS:] = (
@@ -276,25 +309,29 @@
                     x_wide = x_next.astype(F32)
                     acc[s] += x_wide * x_wide
                     vs[i + 1, k, s] = (gi[i + 1, k, s].astype(F32) * x_wide).astype(BF16)
+
+        def forward(q, carry):
+            ks = [q * step + r for r in range(step)]
+
+            @pl.when(has_prev)
+            def _():
+                for k in ks:
+                    halo_fwd(i, k).wait_recv()
+
+            for k in ks:
+                forward_one(k)
             if i + 1 < LAYERS:
                 @pl.when(has_next)
                 def _():
-                    halo_fwd(i + 1, k).start()
-
-                target, remote, local = arrive(i, k)
-
-                @pl.when(target != c)
-                def _():
-                    remote.start()
-
-                @pl.when(target == c)
-                def _():
-                    local.start()
-            return carry
-
-        lax.fori_loop(0, chunks, forward, 0)
+                    for k in ks:
+                        halo_fwd(i + 1, k).start()
+            return carry
+
+        lax.fori_loop(0, chunks // step, forward, 0)
         if i + 1 < LAYERS:
             share(i + 1, True)
+            if i + 1 in ARRIVE:
+                send_arrive(ARRIVE.index(i + 1))
 
     early = chunks // 2
     for i in reversed(range(LAYERS)):
@@ -353,11 +390,7 @@
         lax.fori_loop(0, early, diagonals, 0)
         acc[...] = jnp.zeros_like(acc)
 
-        def backward(k, carry):
-            @pl.when(has_next)
-            def _():
-                halo_bwd(i, k).wait_recv()
-
+        def backward_one(k):
             gu = grouped(back, i, k, both(gzx.at[i, k]))
             for s in range(SEQS):
                 gu_part = gu[:, s * LANES:(s + 1) * LANES]
@@ -366,10 +399,22 @@
                 gn_part = gu_part * gi[i, k, s].astype(F32)
                 gn[k, s] = gn_part
                 acc[s] += gn_part * normed
-            pltpu.make_async_copy(ggi.at[i, k], ggi_out.at[i, :, :, cols(k)], out_sem.at[LAYERS + i]).start()
-            return carry
-
-        lax.fori_loop(0, chunks, backward, 0)
+
+        def backward(q, carry):
+            ks = [q * step + r for r in range(step)]
+
+            @pl.when(has_next)
+            def _():
+                for k in ks:
+                    halo_bwd(i, k).wait_recv()
+
+            for k in ks:
+                backward_one(k)
+            for k in ks:
+                pltpu.make_async_copy(ggi.at[i, k], ggi_out.at[i, :, :, cols(k)], out_sem.at[LAYERS + i]).start()
+            return carry
+
+        lax.fori_loop(0, chunks // step, backward, 0)
         share(ph, False)
         lax.fori_loop(early, chunks, diagonals, 0)
         per = ROWS // n
@@ -420,6 +465,7 @@
         wait_bytes(frecv.at[i, pl.ds(0, n - 1)], fr.at[i])
         gf_out[i] = jnp.sum(frecv[i], axis=0)
 
+    swap().wait_send()
     for i in range(LAYERS):
         wait_bytes(ggo.at[i], out_sem.at[i])
         wait_bytes(ggi.at[i], out_sem.at[LAYERS + i])
@@ -508,6 +554,7 @@
             pltpu.VMEM((LAYERS, chunks) + wide, BF16),
             pltpu.VMEM((LAYERS, chunks) + block, F32),
             pltpu.VMEM((SEQS, ROWS, width), BF16),
+            pltpu.VMEM((SEQS, ROWS // 2, width), BF16),
             pltpu.VMEM((LAYERS, chunks) + wide, BF16),
             pltpu.VMEM((chunks,) + block, F32),
             pltpu.VMEM((LAYERS, chunks) + block, BF16),
@@ -529,7 +576,7 @@
             dma((LAYERS, chunks)), dma((LAYERS, chunks)),
             dma((2 * LAYERS, 2 * nh)), dma((2 * LAYERS,)), dma((2 * LAYERS,)),
             dma((LAYERS,)), dma((LAYERS,)),
-            dma((2, chunks)), dma((2, chunks)),
+            dma((2, chunks)), dma((2, chunks)), dma((2,)),
             dma((2, chunks)), dma((2, chunks)),
             dma((2 * LAYERS,)),
         ],

time: 118 us -> 105 us (0.89)
  Pallas kernels: 116 us -> 104 us
    pallas_call x1, Pallas kernels: 112 us -> 99.4 us  [local(): pl.pallas_call(functools.partial(kernel, n, nh, width), out_shape=(jax.Sh...]
where the time goes in v3:
time: 105 us; the launch traced here: 104 us
  Pallas kernels  104 us (99%)
    pallas_call x1, Pallas kernels, local(): pl.pallas_call(functools.partial(kernel, n, nh, width), out_shape=(jax.Sh...  99.4 us
    pallas_call x1, Pallas kernels, local(): pl.pallas_call(functools.partial(hand_over, per, groups), out_shape=(jax....  4.3 us

profile of v3, /device:TPU:16, one launch (start us, length us, event | category | flops | bytes accessed | tf_op | source)
XLA Modules:
  0.0 104.3 jit_solution(17093326041457236921)
XLA Ops:
  0.6 99.4 %shard_map.84 = (bf16[2,128,1024]{2,1,0:T(8,128)(2,1)}, bf16[3,2,128,1024]{3,2,1,0:T(8,128)(2,1)}, bf16[3,2,128,1024]{3,2,1,0:T(8,128)(2,1)}, f32[3,2,128]{2,1,0:T(2,128)}) custom-call(bf16[2,128,1024]{2,1,0:T(8,128)(2,1)} %act.1, bf16[2,128,1024]{2,1,0:T(8,128)(2,1)} %gin.1, bf16[3,2,128,1024]{3,2,1,0:T(8,128)(2,1)} %go_hbm.1, ...), custom_call_target="tpu_custom_call" | custom-call | tf_op jit(solution)/shard_map/pallas_call | solution.py:538
  100.1 4.3 %shard_map.85 = (bf16[2,128,1024]{2,1,0:T(8,128)(2,1)}, bf16[3,2,128,1024]{3,2,1,0:T(8,128)(2,1)}, bf16[3,2,128,1024]{3,2,1,0:T(8,128)(2,1)}, f32[3,4,64]{2,1,0:T(4,128)}) custom-call(bf16[2,128,1024]{2,1,0:T(8,128)(2,1)} %get-tuple-element.12.a, bf16[3,2,128,1024]{3,2,1,0:T(8,128)(2,1)} %get-tuple-element.13.b, ...), custom_call_target="tpu_custom_call" | custom-call | tf_op jit(solution)/shard_map/pallas_call | solution.py:586

commit v4 on v3

--- a/solution.py
+++ b/solution.py
@@ -509,8 +509,10 @@
 
 
 def hand_over(per, groups, a, b, c, d, a_out, b_out, c_out, d_out, held, get, put):
-    pairs = [(a, a_out)] + [(b.at[i], b_out.at[i]) for i in range(LAYERS)]
-    pairs += [(c.at[i], c_out.at[i]) for i in range(LAYERS)]
+    pairs = [(a.at[s], a_out.at[s]) for s in range(SEQS)]
+    for i in range(LAYERS):
+        for s in range(SEQS):
+            pairs += [(b.at[i, s], b_out.at[i, s]), (c.at[i, s], c_out.at[i, s])]
     for j, (src, _) in enumerate(pairs):
         pltpu.make_async_copy(src, held.at[j], get.at[j]).start()
     half = per // 2
@@ -594,8 +596,8 @@
         in_specs=[any_spec] * 3 + [vmem_spec],
         out_specs=(any_spec, any_spec, any_spec, vmem_spec),
         scratch_shapes=[
-            pltpu.VMEM((2 * LAYERS + 1,) + activations.shape, BF16),
-            dma((2 * LAYERS + 1,)), dma((2 * LAYERS + 1,)),
+            pltpu.VMEM((SEQS * (2 * LAYERS + 1),) + activations.shape[1:], BF16),
+            dma((SEQS * (2 * LAYERS + 1),)), dma((SEQS * (2 * LAYERS + 1),)),
         ],
     )(grad_input, ggo, ggi, lags)
     return grad_input, ggo, ggi, grad_filters.transpose(0, 2, 1)

time: 105 us -> 106 us (level)
  no operation moved by 1% of the time
where the time goes in v4:
time: 106 us; the launch traced here: 105 us
  Pallas kernels  104 us (98%)
    pallas_call x1, Pallas kernels, local(): pl.pallas_call(functools.partial(kernel, n, nh, width), out_shape=(jax.Sh...  99.4 us
    pallas_call x1, Pallas kernels, local(): pl.pallas_call(functools.partial(hand_over, per, groups), out_shape=(jax....  4.53 us

profile of v4, /device:TPU:16, one launch (start us, length us, event | category | flops | bytes accessed | tf_op | source)
XLA Modules:
  0.0 104.6 jit_solution(13512114965072016635)
XLA Ops:
  0.6 99.4 %shard_map.84 = (bf16[2,128,1024]{2,1,0:T(8,128)(2,1)}, bf16[3,2,128,1024]{3,2,1,0:T(8,128)(2,1)}, bf16[3,2,128,1024]{3,2,1,0:T(8,128)(2,1)}, f32[3,2,128]{2,1,0:T(2,128)}) custom-call(bf16[2,128,1024]{2,1,0:T(8,128)(2,1)} %act.1, bf16[2,128,1024]{2,1,0:T(8,128)(2,1)} %gin.1, bf16[3,2,128,1024]{3,2,1,0:T(8,128)(2,1)} %go_hbm.1, ...), custom_call_target="tpu_custom_call" | custom-call | tf_op jit(solution)/shard_map/pallas_call | solution.py:540
  100.1 4.5 %shard_map.85 = (bf16[2,128,1024]{2,1,0:T(8,128)(2,1)}, bf16[3,2,128,1024]{3,2,1,0:T(8,128)(2,1)}, bf16[3,2,128,1024]{3,2,1,0:T(8,128)(2,1)}, f32[3,4,64]{2,1,0:T(4,128)}) custom-call(bf16[2,128,1024]{2,1,0:T(8,128)(2,1)} %get-tuple-element.12.a, bf16[3,2,128,1024]{3,2,1,0:T(8,128)(2,1)} %get-tuple-element.13.b, ...), custom_call_target="tpu_custom_call" | custom-call | tf_op jit(solution)/shard_map/pallas_call | solution.py:588
